TPU v7x, 32 devices: a whole 2x2x4 slice. The times are simulated.
32 devices in a mesh: slide: 4 (over x, core), rows: 8 (over z, y).
Axes of the slice: x: 2, y: 2, z: 4, core: 2. Of those that a mesh axis runs over, the one named last changes fastest.
Arguments:
- features: bfloat16 [4, 192, 256, 128], P('slide', None, 'rows'), may hold values from -6 to 6
- depth_kernel: float32 [192, 49], replicated, may hold values from -0.875 to 0.875
- depth_bias: float32 [192], replicated, may hold values from -4 to 4
- norm_gain: float32 [192], replicated, may hold values from 0.1 to 1.9
- norm_bias: float32 [192], replicated, may hold values from -3 to 3
- up_weight: bfloat16 [192, 768], replicated, may hold values from -0.4375 to 0.4375
- up_bias: float32 [768], replicated, may hold values from -3 to 3
- down_weight: bfloat16 [768, 192], replicated, may hold values from -0.21875 to 0.21875
- down_bias: float32 [192], replicated, may hold values from -4 to 4
- layer_scale: float32 [192], replicated, may hold values from 0.2 to 1
- tissue: int32 [4, 8, 4], P('slide', 'rows'), may hold values 0 or 1
- aggregator_order: int32 [4, 32], P('slide'), may hold values from 0 to 31, each once within a row
- tile_cotangent: bfloat16 [4, 32, 192], P('slide', 'rows'), may hold values from -6 to 6
Outputs:
- embedding: float32 [4, 32, 192], P('slide', 'rows')
- input_grad: bfloat16 [4, 192, 256, 128], P('slide', None, 'rows')
- grad_up: float32 [192, 768], replicated
- grad_down: float32 [768, 192], replicated
- grad_kernel: float32 [192, 49], replicated
Inputs may be any that keep to these rules, and one draw needn't show every extreme that they name: `aggregator_order`: each slide's row is a permutation of the 32 positions.
All inputs are finite; a program needn't handle non-finite values. No bound on the sum of `tissue` on one device may be relied on, other than what follows from the above.
Results may differ from a plain program's by a relative error of at most 0.0064.
Values may be sent and summed in bfloat16 or wider, within the bound.
A program may use at most 128 MiB of HBM per device.

v0:
```python
import math
import jax
import jax.numpy as jnp
from jax import lax
from jax.sharding import PartitionSpec as P

TILE = 32


def extended_2(cells, sides, width):
    for axis, dim in sides:
        count = lax.axis_size(axis)
        ends = count - 1
        head = lax.slice_in_dim(cells, 0, width, axis=dim)
        tail = lax.slice_in_dim(cells, cells.shape[dim] - width, cells.shape[dim], axis=dim)
        cells = jnp.concatenate(
            [
                lax.ppermute(tail, axis, [(i, (i + 1) % count) for i in range(ends)]),
                cells,
                lax.ppermute(head, axis, [((i + 1) % count, i) for i in range(ends)]),
            ],
            axis=dim,
        )
    return cells


def depthwise(source, kernel, height, across, mirrored):
    channels = source.shape[0]
    total = jnp.zeros((channels, height, across), jnp.float32)
    for position in range(49):
        row_start = position // 7
        col_start = position % 7
        if mirrored:
            row_start = 6 - row_start
            col_start = 6 - col_start
        window = lax.slice(
            source, (0, row_start, col_start), (channels, row_start + height, col_start + across)
        )
        total = total + kernel[:, position][:, None, None] * window.astype(jnp.float32)
    return total


def gelu_exact(values):
    return 0.5 * values * (1.0 + jax.scipy.special.erf(values * 0.7071067811865476))


def gelu_slope(values):
    cumulative = 0.5 * (1.0 + jax.scipy.special.erf(values * 0.7071067811865476))
    density = jnp.exp(-0.5 * values * values) * 0.3989422804014327
    return cumulative + values * density


def contract_first(left, right):
    return lax.dot_general(
        left, right, (((0,), (0,)), ((), ())), preferred_element_type=jnp.float32
    )


def contract_last(left, right):
    return lax.dot_general(
        left, right, (((1,), (1,)), ((), ())), preferred_element_type=jnp.float32
    )


def block_pass(
    conv_flat,
    image_flat,
    pixel_mask,
    pixel_cotangent,
    norm_gain,
    norm_bias,
    up_weight,
    up_bias,
    down_weight,
    down_bias,
    layer_scale,
):
    average = jnp.mean(conv_flat, axis=0, keepdims=True)
    centered = conv_flat - average
    variance = jnp.mean(centered * centered, axis=0, keepdims=True)
    reciprocal = lax.rsqrt(variance + 1e-06)
    standard = centered * reciprocal
    normed = (standard * norm_gain[:, None] + norm_bias[:, None]).astype(jnp.bfloat16)
    activation_in = contract_first(up_weight, normed) + up_bias[:, None]
    hidden = gelu_exact(activation_in).astype(jnp.bfloat16)
    branch = contract_first(down_weight, hidden) + down_bias[:, None]
    scaled_mask = pixel_mask[None, :] * layer_scale[:, None]
    output = image_flat.astype(jnp.float32) + scaled_mask * branch
    grad_branch = (scaled_mask * pixel_cotangent).astype(jnp.bfloat16)
    grad_hidden = jnp.dot(down_weight, grad_branch, preferred_element_type=jnp.float32)
    grad_activation = (grad_hidden * gelu_slope(activation_in)).astype(jnp.bfloat16)
    grad_normed = jnp.dot(up_weight, grad_activation, preferred_element_type=jnp.float32)
    grad_standard = grad_normed * norm_gain[:, None]
    grad_conv = reciprocal * (
        grad_standard
        - jnp.mean(grad_standard, axis=0, keepdims=True)
        - standard * jnp.mean(grad_standard * standard, axis=0, keepdims=True)
    )
    grad_conv = grad_conv.astype(jnp.bfloat16)
    up_term = contract_last(normed, grad_activation)
    down_term = contract_last(grad_branch, hidden)
    return (output, grad_conv, up_term, down_term)


def on_device(
    features,
    depth_kernel,
    depth_bias,
    norm_gain,
    norm_bias,
    up_weight,
    up_bias,
    down_weight,
    down_bias,
    layer_scale,
    tissue,
    aggregator_order,
    tile_cotangent,
):
    pixels_in = features[0]
    channels, height, across = pixels_in.shape
    tile_size = TILE
    tiles_here = across // tile_size
    hidden_units = up_weight.shape[1]
    extended = extended_2(pixels_in, (("rows", 1),), 3)
    extended = jnp.pad(extended, ((0, 0), (0, 0), (3, 3)))
    convolved = depthwise(extended, depth_kernel, height, across, False) + depth_bias[:, None, None]
    tile_masks = tissue[0, 0].astype(jnp.float32)
    pixel_mask = jnp.broadcast_to(
        tile_masks[None, :, None], (height, tiles_here, tile_size)
    ).reshape(height * across)
    gathered = lax.all_gather(tile_cotangent, "rows", axis=1, tiled=True)[0]
    positions = lax.dynamic_slice_in_dim(
        aggregator_order[0], lax.axis_index("rows") * tiles_here, tiles_here
    )
    wanted = jnp.take(gathered, positions, axis=0).astype(jnp.float32)
    pixel_cotangent = jnp.broadcast_to(
        wanted.T[:, None, :, None], (channels, height, tiles_here, tile_size)
    ).reshape(channels, height * across)
    output, grad_conv, up_term, down_term = block_pass(
        convolved.reshape(channels, height * across),
        pixels_in.reshape(channels, height * across),
        pixel_mask,
        pixel_cotangent,
        norm_gain,
        norm_bias,
        up_weight,
        up_bias,
        down_weight,
        down_bias,
        layer_scale,
    )
    embedding = jnp.mean(output.reshape(channels, height, tiles_here, tile_size), axis=(1, 3)).T[
        None
    ]
    grad_image = grad_conv.reshape(channels, height, across)
    grad_extended = extended_2(grad_image, (("rows", 1),), 3)
    grad_extended = jnp.pad(grad_extended, ((0, 0), (0, 0), (3, 3)))
    backward_conv = depthwise(grad_extended, depth_kernel, height, across, True)
    input_grad = (pixel_cotangent.reshape(channels, height, across) + backward_conv).astype(
        jnp.bfloat16
    )[None]
    kernel_cols = []
    for position in range(49):
        row_start = position // 7
        col_start = position % 7
        window = lax.slice(
            extended, (0, row_start, col_start), (channels, row_start + height, col_start + across)
        )
        kernel_cols.append(
            jnp.einsum("chw,chw->c", grad_image, window, preferred_element_type=jnp.float32)
        )
    kernel_term = jnp.stack(kernel_cols, axis=1)
    loss_norm = 1.0 / math.sqrt(lax.axis_size("slide") * lax.axis_size("rows") * height * across)
    combined = (
        jnp.concatenate(
            [up_term, down_term, kernel_term, jnp.zeros((channels, 15), jnp.float32)], axis=1
        )
        * loss_norm
    )
    totals = lax.psum(combined, ("slide", "rows"))
    grad_up = totals[:, :hidden_units]
    grad_down = totals[:, hidden_units : 2 * hidden_units].T
    grad_kernel = totals[:, 2 * hidden_units : 2 * hidden_units + 49]
    return (embedding, input_grad, grad_up, grad_down, grad_kernel)


def solution(mesh):
    return jax.shard_map(
        on_device,
        mesh=mesh,
        in_specs=(
            P("slide", None, "rows", None),
            P(),
            P(),
            P(),
            P(),
            P(),
            P(),
            P(),
            P(),
            P(),
            P("slide", "rows", None),
            P("slide", None),
            P("slide", "rows", None),
        ),
        out_specs=(P("slide", "rows", None), P("slide", None, "rows", None), P(), P(), P()),
        check_vma=False,
    )
```

profile of v0, /device:TPU:0, one launch (start us, length us, event | category | flops | bytes accessed | tf_op | source)
XLA Modules:
  0.0 483.2 jit_solution(3109074101789072919)
XLA Ops:
  8.6 4.9 %collective-permute-start = (bf16[192,3,128]{2,1,0:T(4,128)(2,1)S(1)}, bf16[192,3,128]{2,1,0:T(4,128)(2,1)S(1)}, u32[]{:S(2)}, u32[]{:S(2)}) collective-permute-start(bf16[192,3,128]{2,1,0:T(4,128)(2,1)S(1)} %get-tuple-element.81), channel_id=1, source_target_pairs={{0,1},{1,2},{2,3},{3,4},{4,5},{5,6},{6,7},{8,9},{9,10},{10,11},{11... | collective-permute-start | bytes 442376 | tf_op jit(solution)/shard_map/ppermute | solution.py:18
  16.0 1.6 fusion.164
  20.0 32.9 %all_gather.3 = bf16[1,32,192]{2,0,1:T(2,128)(2,1)S(1)} all-gather(bf16[1,4,192]{2,0,1:T(2,128)(2,1)S(1)} %copy.129), channel_id=1, replica_groups=mesh['slide'=4,'rows'=8] {'rows'}, dimensions={1}, use_global_device_ids=true | all-gather | bytes 13824 | tf_op jit(solution)/shard_map/all_gather | solution.py:132
  53.6 2.4 broadcast_in_dim.55
  56.0 5.4 %copy.131 = f32[192,4096]{1,0:T(8,128)} copy(f32[192,4096]{0,1:T(8,128)} %bitcast.261) | data formatting | bytes 6291456 | tf_op jit(solution)/shard_map/reshape | solution.py:139
  61.8 2.1 convert.150
  63.9 1.5 fusion.165
  65.5 4.7 select_maximum_fusion.2
  70.6 95.8 %fusion.159 = (f32[32,128]{1,0:T(8,128)S(1)}, f32[192,32,128]{2,1,0:T(8,128)}) fusion(f32[192]{0:T(256)S(1)} %copy-done.71, bf16[192,38,134]{2,1,0:T(8,128)(2,1)} %select_maximum_fusion.2, f32[192]{0:T(256)} %bitcast.50, f32[192]{0:T(256)} %bitcast.49, f32[192]{0:T(256)S(1)} %bitcast.266, bf16[192,3,128]{2,1,0:T(4,128)(2,1)S(1)} %collective-permute-done.1, ...), kind=kLoop, calls=%fused_computation.307 | loop fusion | flops 130543616 | bytes 71128576 | tf_op jit(solution)/shard_map/reduce_sum | solution.py:78
  166.5 2.4 multiply_reduce_fusion
  169.3 7.6 %fusion.7 = (bf16[768,4096]{0,1:T(8,128)(2,1)}, f32[4096,768]{1,0:T(8,128)S(1)}) fusion(f32[768]{0:T(1024)S(1)} %copy-done.72, bf16[192,768]{1,0:T(8,128)(2,1)S(1)} %copy-done, f32[24,8,32,128]{3,2,1,0:T(8,128)S(1)} %bitcast.252, f32[192]{0:T(256)S(1)} %copy-done.73, f32[192]{0:T(256)S(1)} %copy-done.69, f32[4096]{0:T(1024)S(1)} %rsqrt_bitcast_fusion, ...), kind=kOutput, calls=%fused_computation.61 | convolution fusion | flops 1230766080 | bytes 22352384 | tf_op jit(solution)/shard_map/dot_general | solution.py:54
  176.9 7.0 %fusion.5 = bf16[768,4096]{0,1:T(8,128)(2,1)S(1)} fusion(f32[4096,768]{1,0:T(8,128)S(1)} %get-tuple-element.137, bf16[768,192]{0,1:T(8,128)(2,1)S(1)} %copy-done.15, f32[768]{0:T(1024)S(1)} %copy-done.72, f32[192,4096]{1,0:T(8,128)S(1)} %copy-done.6, f32[192]{0:T(256)S(1)} %copy-done.67, f32[4096]{0:T(1024)S(1)} %mul.896), kind=kOutput, calls=%fused_computation.57 | convolution fusion | flops 1244921856 | bytes 22335232 | tf_op jit(solution)/shard_map/dot_general | solution.py:90
  183.9 3.8 fusion.157
  187.7 5.1 %fusion.142 = (f32[4096]{0:T(1024)S(1)}, f32[4096,192]{0,1:T(8,128)}) fusion(f32[24,8,32,128]{3,2,1,0:T(8,128)S(1)} %bitcast.254, f32[4096]{0:T(1024)S(1)} %rsqrt_bitcast_fusion, f32[4096]{0:T(1024)S(1)} %get-tuple-element.134, f32[192]{0:T(256)S(1)} %copy-done.69, bf16[768,4096]{0,1:T(8,128)(2,1)S(1)} %fusion.5, bf16[192,768]{1,0:T(8,128)(2,1)S(1)} %copy-done), kind=kOutput, calls=%fused_computation.257 | convolution fusion | flops 1211887616 | bytes 12927744 | tf_op jit(solution)/shard_map/dot_general | solution.py:92
  192.9 2.0 reduce_sum.48
  194.9 6.1 %fusion.150 = bf16[24,8,32,128]{3,1,2,0:T(8,128)(2,1)S(1)} fusion(f32[24,8,32,128]{3,2,1,0:T(8,128)} %bitcast.251, f32[4096,192]{0,1:T(8,128)} %get-tuple-element.139, f32[4096]{0:T(1024)S(1)} %get-tuple-element.140, f32[4096]{0:T(1024)S(1)} %get-tuple-element.141, f32[4096]{0:T(1024)S(1)} %rsqrt_bitcast_fusion, f32[4096]{0:T(1024)S(1)} %get-tuple-element.134), kind=kLoop, calls=%fused_computation.280 | loop fusion | flops 5505024 | bytes 7929856
  201.4 22.0 %fusion.116 = (f32[192]{0:T(256)}, f32[192]{0:T(256)}, f32[192]{0:T(256)}, f32[192]{0:T(256)}, f32[192]{0:T(256)}, /*index=5*/f32[192]{0:T(256)}, f32[192]{0:T(2...) fusion(bf16[192,38,134]{2,1,0:T(8,128)(2,1)S(1)} %copy-done.2, ...), kind=kLoop, calls=%fused_computation.228 | loop fusion | flops 43250304 | bytes 29898240 | tf_op jit(solution)/shard_map/chw,chw->c/dot_general | solution.py:171
  223.4 22.2 %fusion.137 = (f32[192]{0:T(256)}, f32[192]{0:T(256)}, f32[192]{0:T(256)}, f32[192]{0:T(256)}, f32[192]{0:T(256)}, /*index=5*/f32[192]{0:T(256)}, f32[192]{0:T(2...) fusion(bf16[192,38,134]{2,1,0:T(8,128)(2,1)S(1)} %copy-done.2, ...), kind=kLoop, calls=%fused_computation.249 | loop fusion | flops 43250304 | bytes 29898240 | tf_op jit(solution)/shard_map/chw,chw->c/dot_general | solution.py:171
  245.6 6.3 %fusion.95 = (f32[192]{0:T(256)}, f32[192]{0:T(256)}, f32[192]{0:T(256)}, f32[192]{0:T(256)}, f32[192]{0:T(256)}, /*index=5*/f32[192]{0:T(256)}) fusion(bf16[192,38,134]{2,1,0:T(8,128)(2,1)S(1)} %copy-done.2, bf16[24,8,32,128]{3,2,1,0:T(8,128)(2,1)S(1)} %copy.430), kind=kLoop, calls=%fused_computation.207 | loop fusion | flops 14941056 | bytes 11014656 | tf_op jit(solution)/shard_map/chw,chw->c/dot_general | solution.py:171
  255.5 1.4 copy.143
  257.0 1.4 copy.144
  258.4 1.4 copy.145
  259.8 1.4 copy.146
  261.3 1.4 copy.147
  265.5 1.4 copy.151
  268.3 1.4 copy.153
  269.7 1.4 copy.154
  273.9 1.4 copy.158
  275.3 1.4 copy.159
  278.1 1.4 copy.161
  279.5 1.4 copy.162
  280.9 1.4 copy.164
  282.4 1.4 copy.165
  285.1 1.4 copy.167
  286.6 1.4 copy.168
  288.0 1.4 copy.169
  290.8 1.4 copy.172
  292.2 1.4 copy.173
  293.7 1.4 copy.174
  295.1 1.4 copy.175
  296.5 1.4 copy.176
  298.0 1.4 copy.178
  299.4 1.4 copy.179
  300.9 1.4 copy.180
  302.3 1.4 copy.132
  303.7 1.4 copy.133
  309.3 1.4 copy.138
  310.7 7.6 %fusion.134 = (f32[192]{0:T(256)}, f32[192]{0:T(256)}, f32[192]{0:T(256)}, f32[192]{0:T(256)}, f32[192]{0:T(256)}, /*index=5*/f32[192]{0:T(256)}, f32[192]{0:T(256)}) fusion(bf16[192,3,128]{2,1,0:T(4,128)(2,1)} %copy-done.9, bf16[192,32,128]{2,1,0:T(8,128)(2,1)S(1)} %bitcast.259, bf16[24,8,32,128]{3,2,1,0:T(8,128)(2,1)S(1)} %copy.430, ...), kind=kLoop, calls=%fused_computation.246 | loop fusion | flops 31455936 | bytes 5018880 | tf_op jit(solution)/shard_map/chw,chw->c/dot_general | solution.py:171
  318.3 1.4 copy.135
  319.8 1.4 copy.142
  321.2 1.4 copy.149
  324.0 1.4 copy.163
  325.4 1.4 copy.170
  326.8 1.4 copy.177
  328.3 6.1 %fusion.154 = f32[192,768]{1,0:T(8,128)} fusion(bf16[768,4096]{0,1:T(8,128)(2,1)} %get-tuple-element.136, f32[192,4096]{1,0:T(8,128)} %copy.131, f32[192]{0:T(256)} %param.22, f32[4096]{0:T(1024)S(1)} %mul.896), kind=kOutput, calls=%fused_computation.304 | convolution fusion | flops 1210318848 | bytes 10044160 | tf_op jit(solution)/shard_map/dot_general | solution.py:60
  335.0 4.0 concatenate.35
  342.4 4.8 collective-permute-start.2
  347.2 9.0 %fusion.13 = f32[192,4096]{1,0:T(8,128)} fusion(bf16[768,4096]{0,1:T(8,128)(2,1)} %get-tuple-element.136, bf16[768,192]{0,1:T(8,128)(2,1)} %param.20, f32[24,8,32,128]{3,2,1,0:T(8,128)} %convert.150, f32[192]{0:T(256)S(1)} %copy-done.70, f32[192]{0:T(256)S(1)} %copy-done.68, f32[4096]{0:T(1024)S(1)} %mul.896), kind=kOutput, calls=%fused_computation.71 | convolution fusion | flops 1211105280 | bytes 12895744 | tf_op jit(solution)/shard_map/dot_general | solution.py:54
  356.1 5.1 %copy.128 = f32[192,4096]{0,1:T(8,128)} copy(f32[192,4096]{1,0:T(8,128)} %fusion.13) | data formatting | bytes 6291456 | tf_op jit(solution)/shard_map/add | solution.py:88
  361.3 2.6 reduce_sum.47
  365.1 3.4 select_maximum_fusion
  368.6 46.0 %fusion.151 = bf16[1,192,32,128]{3,2,1,0:T(8,128)(2,1)} fusion(bf16[192,38,134]{2,1,0:T(8,128)(2,1)S(1)} %select_maximum_fusion, f32[192]{0:T(256)} %bitcast.50, f32[192]{0:T(256)} %bitcast.49, f32[192]{0:T(256)S(1)} %bitcast.267, bf16[192,32,128]{2,1,0:T(8,128)(2,1)S(1)} %bitcast.250, bf16[192,3,128]{2,1,0:T(4,128)(2,1)S(1)} %collective-permute-done.2, ...), kind=kLoop, calls=%fused_computation.284 | loop fusion | flops 123469824 | bytes 74208000 | tf_op jit(solution)/shard_map/broadcast_in_dim | solution.py:160
  414.7 57.5 %all-reduce.4.cloned.1.call-done = f32[192,1600]{1,0:T(8,128)} async-done(((f32[192,1600]{1,0:T(8,128)}), f32[192,1600]{1,0:T(8,128)}) %all-reduce.4.cloned.1.call-update) | async-done | bytes 1228816 | tf_op jit(solution)/shard_map/psum | solution.py:181
  473.8 2.3 slice_bitcast_fusion
  (199 shorter events, 34.6 us)
Async XLA Ops:
  7.2 161.8 %copy-start = (bf16[192,768]{1,0:T(8,128)(2,1)S(1)}, bf16[192,768]{1,0:T(8,128)(2,1)}, u32[]{:S(2)}) copy-start(bf16[192,768]{1,0:T(8,128)(2,1)} %param.18) | copy-start | bytes 884740
  7.2 465.0 %all-reduce.4.cloned.1.call-start = ((), (), s32[]{:S(2)}) async-start(), calls=%async_computation | async-start | bytes 2555904 | tf_op jit(solution)/shard_map/psum | solution.py:181
  8.6 56.9 %collective-permute-start = (bf16[192,3,128]{2,1,0:T(4,128)(2,1)S(1)}, bf16[192,3,128]{2,1,0:T(4,128)(2,1)S(1)}, u32[]{:S(2)}, u32[]{:S(2)}) collective-permute-start(bf16[192,3,128]{2,1,0:T(4,128)(2,1)S(1)} %get-tuple-element.81), channel_id=1, source_target_pairs={{0,1},{1,2},{2,3},{3,4},{4,5},{5,6},{6,7},{8,9},{9,10},{10,11},{11... | collective-permute-start | bytes 442376 | tf_op jit(solution)/shard_map/ppermute | solution.py:18
  13.5 52.0 %collective-permute-start.1 = (bf16[192,3,128]{2,1,0:T(4,128)(2,1)S(1)}, bf16[192,3,128]{2,1,0:T(4,128)(2,1)S(1)}, u32[]{:S(2)}, u32[]{:S(2)}) collective-permute-start(bf16[192,3,128]{2,1,0:T(4,128)(2,1)S(1)} %get-tuple-element.82), channel_id=1, source_target_pairs={{1,0},{2,1},{3,2},{4,3},{5,4},{6,5},{7,6},{9,8},{10,9},{11,10},{12... | collective-permute-start | bytes 442376 | tf_op jit(solution)/shard_map/ppermute | solution.py:20
  15.9 54.4 %copy-start.16 = (f32[192,1]{0,1:T(1,128)}, f32[192,1]{0,1:T(1,128)S(1)}, u32[]{:S(2)}) copy-start(f32[192,1]{0,1:T(1,128)S(1)} %get-tuple-element.85) | copy-start | bytes 2308
  15.9 54.4 %copy-start.18 = (f32[192,1]{0,1:T(1,128)}, f32[192,1]{0,1:T(1,128)S(1)}, u32[]{:S(2)}) copy-start(f32[192,1]{0,1:T(1,128)S(1)} %get-tuple-element.86) | copy-start | bytes 2308
  15.9 54.4 %copy-start.20 = (f32[192,1]{0,1:T(1,128)}, f32[192,1]{0,1:T(1,128)S(1)}, u32[]{:S(2)}) copy-start(f32[192,1]{0,1:T(1,128)S(1)} %get-tuple-element.87) | copy-start | bytes 2308
  15.9 54.4 %copy-start.22 = (f32[192,1]{0,1:T(1,128)}, f32[192,1]{0,1:T(1,128)S(1)}, u32[]{:S(2)}) copy-start(f32[192,1]{0,1:T(1,128)S(1)} %get-tuple-element.88) | copy-start | bytes 2308
  15.9 54.4 %copy-start.24 = (f32[192,1]{0,1:T(1,128)}, f32[192,1]{0,1:T(1,128)S(1)}, u32[]{:S(2)}) copy-start(f32[192,1]{0,1:T(1,128)S(1)} %get-tuple-element.89) | copy-start | bytes 2308
  15.9 54.4 %copy-start.26 = (f32[192,1]{0,1:T(1,128)}, f32[192,1]{0,1:T(1,128)S(1)}, u32[]{:S(2)}) copy-start(f32[192,1]{0,1:T(1,128)S(1)} %get-tuple-element.90) | copy-start | bytes 2308
  15.9 54.4 %copy-start.28 = (f32[192,1]{0,1:T(1,128)}, f32[192,1]{0,1:T(1,128)S(1)}, u32[]{:S(2)}) copy-start(f32[192,1]{0,1:T(1,128)S(1)} %get-tuple-element.91) | copy-start | bytes 2308
  15.9 54.4 %copy-start.30 = (f32[192,1]{0,1:T(1,128)}, f32[192,1]{0,1:T(1,128)S(1)}, u32[]{:S(2)}) copy-start(f32[192,1]{0,1:T(1,128)S(1)} %get-tuple-element.92) | copy-start | bytes 2308
  15.9 54.4 %copy-start.32 = (f32[192,1]{0,1:T(1,128)}, f32[192,1]{0,1:T(1,128)S(1)}, u32[]{:S(2)}) copy-start(f32[192,1]{0,1:T(1,128)S(1)} %get-tuple-element.93) | copy-start | bytes 2308
  15.9 54.4 %copy-start.34 = (f32[192,1]{0,1:T(1,128)}, f32[192,1]{0,1:T(1,128)S(1)}, u32[]{:S(2)}) copy-start(f32[192,1]{0,1:T(1,128)S(1)} %get-tuple-element.94) | copy-start | bytes 2308
  16.0 54.4 %copy-start.36 = (f32[192,1]{0,1:T(1,128)}, f32[192,1]{0,1:T(1,128)S(1)}, u32[]{:S(2)}) copy-start(f32[192,1]{0,1:T(1,128)S(1)} %get-tuple-element.95) | copy-start | bytes 2308
  16.0 54.4 %copy-start.38 = (f32[192,1]{0,1:T(1,128)}, f32[192,1]{0,1:T(1,128)S(1)}, u32[]{:S(2)}) copy-start(f32[192,1]{0,1:T(1,128)S(1)} %get-tuple-element.96) | copy-start | bytes 2308
  16.0 54.4 %copy-start.40 = (f32[192,1]{0,1:T(1,128)}, f32[192,1]{0,1:T(1,128)S(1)}, u32[]{:S(2)}) copy-start(f32[192,1]{0,1:T(1,128)S(1)} %get-tuple-element.97) | copy-start | bytes 2308
  16.0 54.4 %copy-start.42 = (f32[192,1]{0,1:T(1,128)}, f32[192,1]{0,1:T(1,128)S(1)}, u32[]{:S(2)}) copy-start(f32[192,1]{0,1:T(1,128)S(1)} %get-tuple-element.98) | copy-start | bytes 2308
  16.0 54.4 %copy-start.44 = (f32[192,1]{0,1:T(1,128)}, f32[192,1]{0,1:T(1,128)S(1)}, u32[]{:S(2)}) copy-start(f32[192,1]{0,1:T(1,128)S(1)} %get-tuple-element.99) | copy-start | bytes 2308
  16.0 54.4 %copy-start.45 = (f32[192,1]{0,1:T(1,128)}, f32[192,1]{0,1:T(1,128)S(1)}, u32[]{:S(2)}) copy-start(f32[192,1]{0,1:T(1,128)S(1)} %get-tuple-element.100) | copy-start | bytes 2308
  16.0 54.4 %copy-start.46 = (f32[192,1]{0,1:T(1,128)}, f32[192,1]{0,1:T(1,128)S(1)}, u32[]{:S(2)}) copy-start(f32[192,1]{0,1:T(1,128)S(1)} %get-tuple-element.101) | copy-start | bytes 2308
  16.0 54.4 %copy-start.47 = (f32[192,1]{0,1:T(1,128)}, f32[192,1]{0,1:T(1,128)S(1)}, u32[]{:S(2)}) copy-start(f32[192,1]{0,1:T(1,128)S(1)} %get-tuple-element.102) | copy-start | bytes 2308
  16.0 54.4 %copy-start.48 = (f32[192,1]{0,1:T(1,128)}, f32[192,1]{0,1:T(1,128)S(1)}, u32[]{:S(2)}) copy-start(f32[192,1]{0,1:T(1,128)S(1)} %get-tuple-element.103) | copy-start | bytes 2308
  17.6 52.8 %copy-start.49 = (f32[192,1]{0,1:T(1,128)}, f32[192,1]{0,1:T(1,128)S(1)}, u32[]{:S(2)}) copy-start(f32[192,1]{0,1:T(1,128)S(1)} %get-tuple-element.104) | copy-start | bytes 2308
  17.7 52.8 %copy-start.50 = (f32[192,1]{0,1:T(1,128)}, f32[192,1]{0,1:T(1,128)S(1)}, u32[]{:S(2)}) copy-start(f32[192,1]{0,1:T(1,128)S(1)} %get-tuple-element.105) | copy-start | bytes 2308
  17.7 52.8 %copy-start.51 = (f32[192,1]{0,1:T(1,128)}, f32[192,1]{0,1:T(1,128)S(1)}, u32[]{:S(2)}) copy-start(f32[192,1]{0,1:T(1,128)S(1)} %get-tuple-element.106) | copy-start | bytes 2308
  17.7 52.8 %copy-start.52 = (f32[192,1]{0,1:T(1,128)}, f32[192,1]{0,1:T(1,128)S(1)}, u32[]{:S(2)}) copy-start(f32[192,1]{0,1:T(1,128)S(1)} %get-tuple-element.107) | copy-start | bytes 2308
  17.7 52.8 %copy-start.53 = (f32[192,1]{0,1:T(1,128)}, f32[192,1]{0,1:T(1,128)S(1)}, u32[]{:S(2)}) copy-start(f32[192,1]{0,1:T(1,128)S(1)} %get-tuple-element.108) | copy-start | bytes 2308
  17.7 52.8 %copy-start.54 = (f32[192,1]{0,1:T(1,128)}, f32[192,1]{0,1:T(1,128)S(1)}, u32[]{:S(2)}) copy-start(f32[192,1]{0,1:T(1,128)S(1)} %get-tuple-element.109) | copy-start | bytes 2308
  17.7 52.8 %copy-start.55 = (f32[192,1]{0,1:T(1,128)}, f32[192,1]{0,1:T(1,128)S(1)}, u32[]{:S(2)}) copy-start(f32[192,1]{0,1:T(1,128)S(1)} %get-tuple-element.110) | copy-start | bytes 2308
  17.7 52.8 %copy-start.56 = (f32[192,1]{0,1:T(1,128)}, f32[192,1]{0,1:T(1,128)S(1)}, u32[]{:S(2)}) copy-start(f32[192,1]{0,1:T(1,128)S(1)} %get-tuple-element.111) | copy-start | bytes 2308
  17.7 52.8 %copy-start.57 = (f32[192,1]{0,1:T(1,128)}, f32[192,1]{0,1:T(1,128)S(1)}, u32[]{:S(2)}) copy-start(f32[192,1]{0,1:T(1,128)S(1)} %get-tuple-element.112) | copy-start | bytes 2308
  17.7 52.8 %copy-start.58 = (f32[192,1]{0,1:T(1,128)}, f32[192,1]{0,1:T(1,128)S(1)}, u32[]{:S(2)}) copy-start(f32[192,1]{0,1:T(1,128)S(1)} %get-tuple-element.113) | copy-start | bytes 2308
  17.7 52.8 %copy-start.59 = (f32[192,1]{0,1:T(1,128)}, f32[192,1]{0,1:T(1,128)S(1)}, u32[]{:S(2)}) copy-start(f32[192,1]{0,1:T(1,128)S(1)} %get-tuple-element.114) | copy-start | bytes 2308
  17.7 52.8 %copy-start.60 = (f32[192,1]{0,1:T(1,128)}, f32[192,1]{0,1:T(1,128)S(1)}, u32[]{:S(2)}) copy-start(f32[192,1]{0,1:T(1,128)S(1)} %get-tuple-element.115) | copy-start | bytes 2308
  17.8 52.8 %copy-start.61 = (f32[192,1]{0,1:T(1,128)}, f32[192,1]{0,1:T(1,128)S(1)}, u32[]{:S(2)}) copy-start(f32[192,1]{0,1:T(1,128)S(1)} %get-tuple-element.116) | copy-start | bytes 2308
  17.8 52.8 %copy-start.62 = (f32[192,1]{0,1:T(1,128)}, f32[192,1]{0,1:T(1,128)S(1)}, u32[]{:S(2)}) copy-start(f32[192,1]{0,1:T(1,128)S(1)} %get-tuple-element.117) | copy-start | bytes 2308
  17.8 52.8 %copy-start.63 = (f32[192,1]{0,1:T(1,128)}, f32[192,1]{0,1:T(1,128)S(1)}, u32[]{:S(2)}) copy-start(f32[192,1]{0,1:T(1,128)S(1)} %get-tuple-element.118) | copy-start | bytes 2308
  17.8 52.8 %copy-start.64 = (f32[192,1]{0,1:T(1,128)}, f32[192,1]{0,1:T(1,128)S(1)}, u32[]{:S(2)}) copy-start(f32[192,1]{0,1:T(1,128)S(1)} %get-tuple-element.119) | copy-start | bytes 2308
  17.8 52.8 %copy-start.65 = (f32[192,1]{0,1:T(1,128)}, f32[192,1]{0,1:T(1,128)S(1)}, u32[]{:S(2)}) copy-start(f32[192,1]{0,1:T(1,128)S(1)} %get-tuple-element.120) | copy-start | bytes 2308
  17.8 52.8 %copy-start.66 = (f32[192,1]{0,1:T(1,128)}, f32[192,1]{0,1:T(1,128)S(1)}, u32[]{:S(2)}) copy-start(f32[192,1]{0,1:T(1,128)S(1)} %get-tuple-element.121) | copy-start | bytes 2308
  56.0 5.4 %copy-start.74 = (s32[1,1,4]{2,1,0:T(1,128)S(1)}, s32[1,1,4]{2,1,0:T(1,128)}, u32[]{:S(2)}) copy-start(s32[1,1,4]{2,1,0:T(1,128)} %param.23) | copy-start | bytes 52
  56.0 5.7 %copy-start.4 = (bf16[1,192,32,128]{3,2,1,0:T(8,128)(2,1)S(1)}, bf16[1,192,32,128]{3,2,1,0:T(8,128)(2,1)}, u32[]{:S(2)}) copy-start(bf16[1,192,32,128]{3,2,1,0:T(8,128)(2,1)} %param.13) | copy-start | bytes 4718596
  63.9 6.7 %copy-start.71 = (f32[192]{0:T(256)S(1)}, f32[192]{0:T(256)}, u32[]{:S(2)}) copy-start(f32[192]{0:T(256)} %param.15) | copy-start | bytes 2308
  65.5 101.0 %copy-start.7 = (bf16[192,3,128]{2,1,0:T(4,128)(2,1)}, bf16[192,3,128]{2,1,0:T(4,128)(2,1)S(1)}, u32[]{:S(2)}) copy-start(bf16[192,3,128]{2,1,0:T(4,128)(2,1)S(1)} %collective-permute-done) | copy-start | bytes 442372
  65.5 100.9 %copy-start.9 = (bf16[192,3,128]{2,1,0:T(4,128)(2,1)}, bf16[192,3,128]{2,1,0:T(4,128)(2,1)S(1)}, u32[]{:S(2)}) copy-start(bf16[192,3,128]{2,1,0:T(4,128)(2,1)S(1)} %collective-permute-done.1) | copy-start | bytes 442372
  169.3 7.6 %copy-start.6 = (f32[192,4096]{1,0:T(8,128)S(1)}, f32[192,4096]{1,0:T(8,128)}, u32[]{:S(2)}) copy-start(f32[192,4096]{1,0:T(8,128)} %copy.131) | copy-start | bytes 9437188
  169.3 7.6 %copy-start.15 = (bf16[768,192]{0,1:T(8,128)(2,1)S(1)}, bf16[768,192]{0,1:T(8,128)(2,1)}, u32[]{:S(2)}) copy-start(bf16[768,192]{0,1:T(8,128)(2,1)} %param.20) | copy-start | bytes 884740
  169.3 7.6 %copy-start.67 = (f32[192]{0:T(256)S(1)}, f32[192]{0:T(256)}, u32[]{:S(2)}) copy-start(f32[192]{0:T(256)} %param.22) | copy-start | bytes 2308
  194.9 6.4 %copy-start.2 = (bf16[192,38,134]{2,1,0:T(8,128)(2,1)S(1)}, bf16[192,38,134]{2,1,0:T(8,128)(2,1)}, u32[]{:S(2)}) copy-start(bf16[192,38,134]{2,1,0:T(8,128)(2,1)} %select_maximum_fusion.2) | copy-start | bytes 5865988
  251.8 58.9 %copy-start.5 = (bf16[1,192,32,128]{3,2,1,0:T(8,128)(2,1)S(1)}, bf16[1,192,32,128]{3,2,1,0:T(8,128)(2,1)}, u32[]{:S(2)}) copy-start(bf16[1,192,32,128]{3,2,1,0:T(8,128)(2,1)} %param.13) | copy-start | bytes 4718596
  251.8 58.9 %copy-start.8 = (bf16[192,3,128]{2,1,0:T(4,128)(2,1)S(1)}, bf16[192,3,128]{2,1,0:T(4,128)(2,1)}, u32[]{:S(2)}) copy-start(bf16[192,3,128]{2,1,0:T(4,128)(2,1)} %copy-done.7) | copy-start | bytes 442372
  328.3 6.7 %copy-start.10 = (f32[192,1]{1,0:T(8,128)S(1)}, f32[192,1]{1,0:T(8,128)}, u32[]{:S(2)}) copy-start(f32[192,1]{1,0:T(8,128)} %copy.140) | copy-start | bytes 2308
  328.3 6.7 %copy-start.11 = (f32[192,1]{1,0:T(8,128)S(1)}, f32[192,1]{1,0:T(8,128)}, u32[]{:S(2)}) copy-start(f32[192,1]{1,0:T(8,128)} %copy.141) | copy-start | bytes 2308
  328.3 6.7 %copy-start.12 = (f32[192,1]{1,0:T(8,128)S(1)}, f32[192,1]{1,0:T(8,128)}, u32[]{:S(2)}) copy-start(f32[192,1]{1,0:T(8,128)} %copy.143) | copy-start | bytes 2308
  328.3 6.7 %copy-start.13 = (f32[192,1]{1,0:T(8,128)S(1)}, f32[192,1]{1,0:T(8,128)}, u32[]{:S(2)}) copy-start(f32[192,1]{1,0:T(8,128)} %copy.144) | copy-start | bytes 2308
  328.3 6.7 %copy-start.14 = (f32[192,1]{1,0:T(8,128)S(1)}, f32[192,1]{1,0:T(8,128)}, u32[]{:S(2)}) copy-start(f32[192,1]{1,0:T(8,128)} %copy.145) | copy-start | bytes 2308
  339.0 8.1 %copy-start.68 = (f32[192]{0:T(256)S(1)}, f32[192]{0:T(256)}, u32[]{:S(2)}) copy-start(f32[192]{0:T(256)} %param.22) | copy-start | bytes 2308
  339.0 8.1 %copy-start.70 = (f32[192]{0:T(256)S(1)}, f32[192]{0:T(256)}, u32[]{:S(2)}) copy-start(f32[192]{0:T(256)} %param.21) | copy-start | bytes 2308
  341.1 23.8 %collective-permute-start.3 = (bf16[192,3,128]{2,1,0:T(4,128)(2,1)}, bf16[192,3,128]{2,1,0:T(4,128)(2,1)S(1)}, u32[]{:S(2)}, u32[]{:S(2)}) collective-permute-start(bf16[192,3,128]{2,1,0:T(4,128)(2,1)} %get-tuple-element.80), channel_id=1, source_target_pairs={{1,0},{2,1},{3,2},{4,3},{5,4},{6,5},{7,6},{9,8},{10,9},{11,10},{12... | collective-permute-start | bytes 442376 | tf_op jit(solution)/shard_map/ppermute | solution.py:20
  342.4 22.7 %collective-permute-start.2 = (bf16[192,3,128]{2,1,0:T(4,128)(2,1)S(1)}, bf16[192,3,128]{2,1,0:T(4,128)(2,1)S(1)}, u32[]{:S(2)}, u32[]{:S(2)}) collective-permute-start(bf16[192,3,128]{2,1,0:T(4,128)(2,1)S(1)} %get-tuple-element.79), channel_id=1, source_target_pairs={{0,1},{1,2},{2,3},{3,4},{4,5},{5,6},{6,7},{8,9},{9,10},{10,11},{11... | collective-permute-start | bytes 442376 | tf_op jit(solution)/shard_map/ppermute | solution.py:18
  364.8 3.7 copy-start.17
  364.8 3.7 copy-start.19
  368.6 107.5 %copy-start.1 = (bf16[192,768]{1,0:T(8,128)(2,1)S(1)}, bf16[192,768]{1,0:T(8,128)(2,1)}, u32[]{:S(2)}) copy-start(bf16[192,768]{1,0:T(8,128)(2,1)} %param.18) | copy-start | bytes 884740
  (16 other events, 55.8 us)
Sparse Core Ops, SparseCore 0:
  340.4 131.7 all-reduce.3
where the time goes:
time: 493 us; the launch traced here: 483 us
  other arithmetic  227 us (46%)
  local copies, waits for them, and re-layouts  99.7 us (20%)
  waiting for transfers between devices  57.5 us (12%)
  matrix products  38.6 us (8%)
  blocking collectives  32.9 us (7%)
  between operations  15.4 us (3%)
  starting transfers between devices  12.3 us (2%)
    reduce_sum x1, other arithmetic, block_pass(): average = jnp.mean(conv_flat, axis=0, keepdims=True)  95.8 us
    another operation x49, local copies, waits for them, and re-layouts, on_device(): kernel_term = jnp.stack(kernel_cols, axis=1)  68.8 us
    dot_general x4, other arithmetic, on_device(): jnp.einsum('chw,chw->c', grad_image, window, preferred_element_type=jnp.f...  58.1 us
    psum x1, waiting for transfers between devices, on_device(): totals = lax.psum(combined, ('slide', 'rows'))  57.5 us
    broadcast_in_dim x1, other arithmetic, on_device(): (pixel_cotangent.reshape(channels, height, across) + backward_conv).astyp...  46 us
    all_gather x1, blocking collectives, on_device(): gathered = lax.all_gather(tile_cotangent, 'rows', axis=1, tiled=True)[0]  32.9 us
    dot_general x2, matrix products, contract_first(): lax.dot_general(left, right, (((0,), (0,)), ((), ())), preferred_element_...  16.6 us
    dot_general x2, matrix products, contract_last(): lax.dot_general(left, right, (((1,), (1,)), ((), ())), preferred_element_...  9.89 us
  transfers between devices with their start and end apart: 5, of which 1 were waited for; matrix products, arithmetic and copies ran while one was open for 18% of the time, Pallas kernels for 0%

commit v1 on v0

--- a/solution.py
+++ b/solution.py
@@ -178,7 +178,7 @@
         )
         * loss_norm
     )
-    totals = lax.psum(combined, ("slide", "rows"))
+    totals = jnp.sum(lax.all_gather(combined, ("slide", "rows")), axis=0)
     grad_up = totals[:, :hidden_units]
     grad_down = totals[:, hidden_units : 2 * hidden_units].T
     grad_kernel = totals[:, 2 * hidden_units : 2 * hidden_units + 49]

time: 493 us -> 589 us (1.19)
  waiting for transfers between devices: 57.5 us -> 156 us
  local copies, waits for them, and re-layouts: 99.7 us -> 77.2 us
  other arithmetic: 227 us -> 249 us
    all_gather x0 -> x1, waiting for transfers between devices: none -> 155 us  [on_device(): totals = jnp.sum(lax.all_gather(combined, ('slide', 'rows')), axis=0)]
    another operation x49 -> x0, local copies, waits for them, and re-layouts: 68.8 us -> none  [on_device(): kernel_term = jnp.stack(kernel_cols, axis=1)]
    psum x1 -> x0, waiting for transfers between devices: 57.5 us -> none  [on_device(): totals = lax.psum(combined, ('slide', 'rows'))]
    concatenate x1 -> x50, local copies, waits for them, and re-layouts: 4 us -> 51.4 us  [on_device(): jnp.concatenate([up_term, down_term, kernel_term, jnp.zeros((channels, 15...]
    reduce_sum x0 -> x1, other arithmetic: none -> 14.9 us  [on_device(): totals = jnp.sum(lax.all_gather(combined, ('slide', 'rows')), axis=0)]
  transfers between devices with their start and end apart: 5 -> 5, of which waited for: 1 -> 3; matrix products, arithmetic and copies ran while one was open for 18% -> 15% of each run, Pallas kernels for 0% -> 0%
where the time goes in v1:
time: 589 us; the launch traced here: 579 us
  other arithmetic  249 us (42%)
  waiting for transfers between devices  156 us (26%)
  local copies, waits for them, and re-layouts  77.2 us (13%)
  matrix products  37.9 us (6%)
  blocking collectives  31.4 us (5%)
  between operations  15.7 us (3%)
  starting transfers between devices  12.7 us (2%)
    all_gather x1, waiting for transfers between devices, on_device(): totals = jnp.sum(lax.all_gather(combined, ('slide', 'rows')), axis=0)  155 us
    reduce_sum x1, other arithmetic, block_pass(): average = jnp.mean(conv_flat, axis=0, keepdims=True)  100 us
    dot_general x4, other arithmetic, on_device(): jnp.einsum('chw,chw->c', grad_image, window, preferred_element_type=jnp.f...  61.8 us
    concatenate x50, local copies, waits for them, and re-layouts, on_device(): jnp.concatenate([up_term, down_term, kernel_term, jnp.zeros((channels, 15...  51.4 us
    broadcast_in_dim x1, other arithmetic, on_device(): (pixel_cotangent.reshape(channels, height, across) + backward_conv).astyp...  44 us
    all_gather x1, blocking collectives, on_device(): gathered = lax.all_gather(tile_cotangent, 'rows', axis=1, tiled=True)[0]  31.4 us
    dot_general x2, matrix products, contract_first(): lax.dot_general(left, right, (((0,), (0,)), ((), ())), preferred_element_...  16.6 us
    reduce_sum x1, other arithmetic, on_device(): totals = jnp.sum(lax.all_gather(combined, ('slide', 'rows')), axis=0)  14.9 us
  transfers between devices with their start and end apart: 5, of which 3 were waited for; matrix products, arithmetic and copies ran while one was open for 15% of the time, Pallas kernels for 0%

profile of v1, /device:TPU:0, one launch (start us, length us, event | category | flops | bytes accessed | tf_op | source)
XLA Modules:
  0.0 579.4 jit_solution(16289628073499132102)
XLA Ops:
  7.2 1.3 fusion.160
  8.6 1.3 collective-permute-start.1
  9.9 5.5 collective-permute-start
  15.4 1.2 fusion.161
  16.7 1.7 fusion.162
  21.4 31.4 %all_gather.7 = bf16[1,32,192]{2,0,1:T(2,128)(2,1)S(1)} all-gather(bf16[1,4,192]{2,0,1:T(2,128)(2,1)S(1)} %copy.131), channel_id=1, replica_groups=mesh['slide'=4,'rows'=8] {'rows'}, dimensions={1}, use_global_device_ids=true | all-gather | bytes 13824 | tf_op jit(solution)/shard_map/all_gather | solution.py:132
  53.5 2.4 broadcast_in_dim.55
  55.9 5.5 copy.133
  61.4 1.6 fusion.163
  63.1 4.7 select_maximum_fusion.2
  67.9 100.0 %fusion.157 = (f32[32,128]{1,0:T(8,128)S(1)}, f32[192,32,128]{2,1,0:T(8,128)S(1)}) fusion(f32[192]{0:T(256)} %param.15, bf16[192,38,134]{2,1,0:T(8,128)(2,1)} %select_maximum_fusion.2, f32[192]{0:T(256)} %bitcast.362, f32[192]{0:T(256)} %bitcast.364, f32[192]{0:T(256)S(1)} %bitcast.270, bf16[192,3,128]{2,1,0:T(4,128)(2,1)} %copy-done.7, ...), kind=kLoop, calls=%fused_computation.307 | loop fusion | flops 130543616 | bytes 71128576 | tf_op jit(solution)/shard_map/reduce_sum | solution.py:78
  168.8 7.6 %fusion.7 = (bf16[768,4096]{0,1:T(8,128)(2,1)}, f32[4096,768]{1,0:T(8,128)S(1)}) fusion(f32[768]{0:T(1024)S(1)} %copy-done.94, bf16[192,768]{1,0:T(8,128)(2,1)S(1)} %copy-done, f32[24,8,32,128]{3,2,1,0:T(8,128)S(1)} %bitcast.255, f32[192]{0:T(256)S(1)} %copy-done.95, f32[192]{0:T(256)S(1)} %copy-done.92, f32[4096]{0:T(1024)S(1)} %rsqrt_bitcast_fusion, ...), kind=kOutput, calls=%fused_computation.61 | convolution fusion | flops 1230766080 | bytes 22352384 | tf_op jit(solution)/shard_map/dot_general | solution.py:54
  176.4 7.0 %fusion.5 = bf16[768,4096]{0,1:T(8,128)(2,1)S(1)} fusion(f32[4096,768]{1,0:T(8,128)S(1)} %get-tuple-element.137, bf16[768,192]{0,1:T(8,128)(2,1)S(1)} %copy-done.12, f32[768]{0:T(1024)S(1)} %copy-done.94, f32[192,4096]{1,0:T(8,128)S(1)} %copy-done.6, f32[192]{0:T(256)S(1)} %copy-done.72, f32[4096]{0:T(1024)S(1)} %mul.903), kind=kOutput, calls=%fused_computation.57 | convolution fusion | flops 1244921856 | bytes 22335232 | tf_op jit(solution)/shard_map/dot_general | solution.py:90
  183.4 5.2 fusion.142
  188.5 3.9 convolution_bitcast_fusion.1
  192.4 2.0 reduce_sum.57
  194.5 6.1 %fusion.150 = bf16[24,8,32,128]{3,1,2,0:T(8,128)(2,1)S(1)} fusion(f32[24,8,32,128]{3,2,1,0:T(8,128)} %bitcast.258, f32[4096,192]{0,1:T(8,128)} %get-tuple-element.139, f32[4096]{0:T(1024)S(1)} %get-tuple-element.140, f32[4096]{0:T(1024)S(1)} %get-tuple-element.141, f32[4096]{0:T(1024)S(1)} %rsqrt_bitcast_fusion, f32[4096]{0:T(1024)S(1)} %get-tuple-element.134), kind=kLoop, calls=%fused_computation.280 | loop fusion | flops 5505024 | bytes 7929856
  201.0 6.3 %fusion.95 = (f32[192]{0:T(256)}, f32[192]{0:T(256)S(1)}, f32[192]{0:T(256)S(1)}, f32[192]{0:T(256)S(1)}, f32[192]{0:T(256)S(1)}, /*index=5*/f32[192]{0:T(256)S(1)}) fusion(bf16[192,38,134]{2,1,0:T(8,128)(2,1)S(1)} %copy-done.2, bf16[24,8,32,128]{3,2,1,0:T(8,128)(2,1)S(1)} %copy.432), kind=kLoop, calls=%fused_computation.207 | loop fusion | flops 14941056 | bytes 11014656 | tf_op jit(solution)/shard_map/chw,chw->c/dot_general | solution.py:171
  207.2 22.2 %fusion.116 = (f32[192]{0:T(256)}, f32[192]{0:T(256)}, f32[192]{0:T(256)}, f32[192]{0:T(256)}, f32[192]{0:T(256)}, /*index=5*/f32[192]{0:T(256)}, f32[192]{0:T(2...) fusion(bf16[192,38,134]{2,1,0:T(8,128)(2,1)S(1)} %copy-done.2, ...), kind=kLoop, calls=%fused_computation.228 | loop fusion | flops 43250304 | bytes 29898240 | tf_op jit(solution)/shard_map/chw,chw->c/dot_general | solution.py:171
  229.4 22.0 %fusion.137 = (f32[192]{0:T(256)S(1)}, f32[192]{0:T(256)S(1)}, f32[192]{0:T(256)S(1)}, f32[192]{0:T(256)S(1)}, f32[192]{0:T(256)}, /*index=5*/f32[192]{0:T(256)}...) fusion(bf16[192,38,134]{2,1,0:T(8,128)(2,1)S(1)} %copy-done.2, ...), kind=kLoop, calls=%fused_computation.249 | loop fusion | flops 43250304 | bytes 29898240 | tf_op jit(solution)/shard_map/chw,chw->c/dot_general | solution.py:171
  251.4 5.2 convolution_bitcast_fusion
  257.2 11.4 %fusion.134 = (f32[192]{0:T(256)}, f32[192]{0:T(256)}, f32[192]{0:T(256)}, f32[192]{0:T(256)}, f32[192]{0:T(256)S(1)}, /*index=5*/f32[192]{0:T(256)}, f32[192]{0:T(256)}) fusion(bf16[192,3,128]{2,1,0:T(4,128)(2,1)S(1)} %copy-done.8, bf16[192,32,128]{2,1,0:T(8,128)(2,1)} %bitcast.261, bf16[24,8,32,128]{3,2,1,0:T(8,128)(2,1)S(1)} %copy.432, ...), kind=kLoop, calls=%fused_computation.246 | loop fusion | flops 31455936 | bytes 5018880 | tf_op jit(solution)/shard_map/chw,chw->c/dot_general | solution.py:171
  269.0 0.8 copy.140
  269.8 1.4 copy.141
  271.2 1.4 copy.142
  272.6 1.4 copy.143
  274.0 1.4 copy.144
  275.4 1.4 copy.145
  276.8 1.4 copy.146
  278.2 1.4 copy.147
  279.6 1.4 copy.148
  281.0 1.4 copy.149
  282.4 1.4 copy.150
  283.8 1.4 copy.151
  285.3 1.4 copy.152
  286.6 1.4 copy.153
  288.1 1.4 copy.154
  289.5 1.4 copy.155
  290.9 1.4 copy.156
  292.3 0.8 copy.157
  293.1 1.4 copy.158
  295.3 0.8 copy.160
  296.8 0.8 copy.162
  299.1 1.4 copy.165
  300.5 0.8 copy.166
  302.1 0.8 copy.168
  303.6 0.8 copy.170
  305.1 1.4 copy.172
  309.6 0.8 copy.177
  311.1 1.4 copy.179
  315.5 4.9 concatenate.195
  320.3 2.5 broadcast_multiply_fusion
  322.9 3.5 convert.150
  326.5 9.1 %fusion.13 = f32[192,4096]{1,0:T(8,128)} fusion(bf16[768,4096]{0,1:T(8,128)(2,1)} %get-tuple-element.136, bf16[768,192]{0,1:T(8,128)(2,1)S(1)} %copy-done.13, f32[24,8,32,128]{3,2,1,0:T(8,128)} %convert.150, f32[192]{0:T(256)S(1)} %copy-done.93, f32[192]{0:T(256)S(1)} %copy-done.73, f32[4096]{0:T(1024)S(1)} %mul.903), kind=kOutput, calls=%fused_computation.71 | convolution fusion | flops 1211105280 | bytes 12895744 | tf_op jit(solution)/shard_map/dot_general | solution.py:54
  335.6 5.1 copy.130
  340.7 2.6 reduce_sum.56
  343.5 1.3 collective-permute-start.3
  344.8 4.6 collective-permute-start.2
  351.2 1.3 copy-done.5
  353.1 3.4 select_maximum_fusion
  356.9 44.0 %fusion.151 = bf16[1,192,32,128]{3,2,1,0:T(8,128)(2,1)} fusion(bf16[192,38,134]{2,1,0:T(8,128)(2,1)S(1)} %select_maximum_fusion, f32[192]{0:T(256)} %bitcast.363, f32[192]{0:T(256)} %bitcast.365, f32[192]{0:T(256)S(1)} %bitcast.271, bf16[192,32,128]{2,1,0:T(8,128)(2,1)S(1)} %bitcast.254, bf16[192,3,128]{2,1,0:T(4,128)(2,1)S(1)} %collective-permute-done.2, ...), kind=kLoop, calls=%fused_computation.284 | loop fusion | flops 123469824 | bytes 74208000 | tf_op jit(solution)/shard_map/broadcast_in_dim | solution.py:160
  400.9 154.8 %all-gather.2.cloned.1.call-done = f32[32,192,1600]{2,1,0:T(8,128)} async-done(((f32[1,192,1600]{2,1,0:T(8,128)}), f32[32,192,1600]{2,1,0:T(8,128)}) %all-gather.2.cloned.1.call-update) | async-done | bytes 39321616 | tf_op jit(solution)/shard_map/all_gather | solution.py:181
  555.7 14.9 %reduce_sum.59 = f32[192,1600]{1,0:T(8,128)S(1)} reduce(f32[32,192,1600]{2,1,0:T(8,128)} %all-gather.2.cloned.1.call-done, f32[]{:T(128)} %constant.18.clone.1), dimensions={0}, to_apply=%region_5.6 | reduce | flops 9523200 | bytes 40550404 | tf_op jit(solution)/shard_map/reduce_sum | solution.py:181
  570.5 1.1 slice_bitcast_fusion
  (242 shorter events, 20.9 us)
Async XLA Ops:
  7.2 161.2 %copy-start = (bf16[192,768]{1,0:T(8,128)(2,1)S(1)}, bf16[192,768]{1,0:T(8,128)(2,1)}, u32[]{:S(2)}) copy-start(bf16[192,768]{1,0:T(8,128)(2,1)} %param.18) | copy-start | bytes 884740
  7.2 548.5 %all-gather.2.cloned.1.call-start = ((), (), s32[]{:S(2)}) async-start(), calls=%async_computation | async-start | bytes 42172416 | tf_op jit(solution)/shard_map/all_gather | solution.py:181
  8.6 54.5 %collective-permute-start.1 = (bf16[192,3,128]{2,1,0:T(4,128)(2,1)S(1)}, bf16[192,3,128]{2,1,0:T(4,128)(2,1)S(1)}, u32[]{:S(2)}, u32[]{:S(2)}) collective-permute-start(bf16[192,3,128]{2,1,0:T(4,128)(2,1)S(1)} %get-tuple-element.82), channel_id=1, source_target_pairs={{1,0},{2,1},{3,2},{4,3},{5,4},{6,5},{7,6},{9,8},{10,9},{11,10},{12... | collective-permute-start | bytes 442376 | tf_op jit(solution)/shard_map/ppermute | solution.py:20
  9.9 53.2 %collective-permute-start = (bf16[192,3,128]{2,1,0:T(4,128)(2,1)S(1)}, bf16[192,3,128]{2,1,0:T(4,128)(2,1)S(1)}, u32[]{:S(2)}, u32[]{:S(2)}) collective-permute-start(bf16[192,3,128]{2,1,0:T(4,128)(2,1)S(1)} %get-tuple-element.81), channel_id=1, source_target_pairs={{0,1},{1,2},{2,3},{3,4},{4,5},{5,6},{6,7},{8,9},{9,10},{10,11},{11... | collective-permute-start | bytes 442376 | tf_op jit(solution)/shard_map/ppermute | solution.py:18
  16.6 51.2 %copy-start.14 = (f32[192,1]{0,1:T(1,128)}, f32[192,1]{0,1:T(1,128)S(1)}, u32[]{:S(2)}) copy-start(f32[192,1]{0,1:T(1,128)S(1)} %get-tuple-element.86) | copy-start | bytes 2308
  16.6 51.2 %copy-start.16 = (f32[192,1]{0,1:T(1,128)}, f32[192,1]{0,1:T(1,128)S(1)}, u32[]{:S(2)}) copy-start(f32[192,1]{0,1:T(1,128)S(1)} %get-tuple-element.87) | copy-start | bytes 2308
  16.6 51.2 %copy-start.18 = (f32[192,1]{0,1:T(1,128)}, f32[192,1]{0,1:T(1,128)S(1)}, u32[]{:S(2)}) copy-start(f32[192,1]{0,1:T(1,128)S(1)} %get-tuple-element.88) | copy-start | bytes 2308
  16.6 51.2 %copy-start.20 = (f32[192,1]{0,1:T(1,128)}, f32[192,1]{0,1:T(1,128)S(1)}, u32[]{:S(2)}) copy-start(f32[192,1]{0,1:T(1,128)S(1)} %get-tuple-element.89) | copy-start | bytes 2308
  16.6 51.2 %copy-start.22 = (f32[192,1]{0,1:T(1,128)}, f32[192,1]{0,1:T(1,128)S(1)}, u32[]{:S(2)}) copy-start(f32[192,1]{0,1:T(1,128)S(1)} %get-tuple-element.90) | copy-start | bytes 2308
  16.6 51.2 %copy-start.24 = (f32[192,1]{0,1:T(1,128)}, f32[192,1]{0,1:T(1,128)S(1)}, u32[]{:S(2)}) copy-start(f32[192,1]{0,1:T(1,128)S(1)} %get-tuple-element.91) | copy-start | bytes 2308
  16.6 51.2 %copy-start.26 = (f32[192,1]{0,1:T(1,128)}, f32[192,1]{0,1:T(1,128)S(1)}, u32[]{:S(2)}) copy-start(f32[192,1]{0,1:T(1,128)S(1)} %get-tuple-element.92) | copy-start | bytes 2308
  16.6 51.2 %copy-start.28 = (f32[192,1]{0,1:T(1,128)}, f32[192,1]{0,1:T(1,128)S(1)}, u32[]{:S(2)}) copy-start(f32[192,1]{0,1:T(1,128)S(1)} %get-tuple-element.93) | copy-start | bytes 2308
  16.6 51.2 %copy-start.30 = (f32[192,1]{0,1:T(1,128)}, f32[192,1]{0,1:T(1,128)S(1)}, u32[]{:S(2)}) copy-start(f32[192,1]{0,1:T(1,128)S(1)} %get-tuple-element.94) | copy-start | bytes 2308
  16.7 51.2 %copy-start.32 = (f32[192,1]{0,1:T(1,128)}, f32[192,1]{0,1:T(1,128)S(1)}, u32[]{:S(2)}) copy-start(f32[192,1]{0,1:T(1,128)S(1)} %get-tuple-element.95) | copy-start | bytes 2308
  16.7 51.2 %copy-start.34 = (f32[192,1]{0,1:T(1,128)}, f32[192,1]{0,1:T(1,128)S(1)}, u32[]{:S(2)}) copy-start(f32[192,1]{0,1:T(1,128)S(1)} %get-tuple-element.96) | copy-start | bytes 2308
  16.7 51.2 %copy-start.36 = (f32[192,1]{0,1:T(1,128)}, f32[192,1]{0,1:T(1,128)S(1)}, u32[]{:S(2)}) copy-start(f32[192,1]{0,1:T(1,128)S(1)} %get-tuple-element.97) | copy-start | bytes 2308
  16.7 51.2 %copy-start.38 = (f32[192,1]{0,1:T(1,128)}, f32[192,1]{0,1:T(1,128)S(1)}, u32[]{:S(2)}) copy-start(f32[192,1]{0,1:T(1,128)S(1)} %get-tuple-element.98) | copy-start | bytes 2308
  16.7 51.2 %copy-start.40 = (f32[192,1]{0,1:T(1,128)}, f32[192,1]{0,1:T(1,128)S(1)}, u32[]{:S(2)}) copy-start(f32[192,1]{0,1:T(1,128)S(1)} %get-tuple-element.99) | copy-start | bytes 2308
  16.7 51.2 %copy-start.42 = (f32[192,1]{0,1:T(1,128)}, f32[192,1]{0,1:T(1,128)S(1)}, u32[]{:S(2)}) copy-start(f32[192,1]{0,1:T(1,128)S(1)} %get-tuple-element.100) | copy-start | bytes 2308
  16.7 51.2 %copy-start.44 = (f32[192,1]{0,1:T(1,128)}, f32[192,1]{0,1:T(1,128)S(1)}, u32[]{:S(2)}) copy-start(f32[192,1]{0,1:T(1,128)S(1)} %get-tuple-element.101) | copy-start | bytes 2308
  16.7 51.2 %copy-start.46 = (f32[192,1]{0,1:T(1,128)}, f32[192,1]{0,1:T(1,128)S(1)}, u32[]{:S(2)}) copy-start(f32[192,1]{0,1:T(1,128)S(1)} %get-tuple-element.102) | copy-start | bytes 2308
  16.7 51.2 %copy-start.48 = (f32[192,1]{0,1:T(1,128)}, f32[192,1]{0,1:T(1,128)S(1)}, u32[]{:S(2)}) copy-start(f32[192,1]{0,1:T(1,128)S(1)} %get-tuple-element.103) | copy-start | bytes 2308
  55.9 7.1 %copy-start.4 = (bf16[1,192,32,128]{3,2,1,0:T(8,128)(2,1)S(1)}, bf16[1,192,32,128]{3,2,1,0:T(8,128)(2,1)}, u32[]{:S(2)}) copy-start(bf16[1,192,32,128]{3,2,1,0:T(8,128)(2,1)} %param.13) | copy-start | bytes 4718596
  167.9 20.6 %copy-start.3 = (f32[192,32,128]{2,1,0:T(8,128)}, f32[192,32,128]{2,1,0:T(8,128)S(1)}, u32[]{:S(2)}) copy-start(f32[192,32,128]{2,1,0:T(8,128)S(1)} %get-tuple-element.78) | copy-start | bytes 9437188
  168.8 7.6 %copy-start.6 = (f32[192,4096]{1,0:T(8,128)S(1)}, f32[192,4096]{1,0:T(8,128)}, u32[]{:S(2)}) copy-start(f32[192,4096]{1,0:T(8,128)} %copy.133) | copy-start | bytes 9437188
  168.8 7.6 %copy-start.12 = (bf16[768,192]{0,1:T(8,128)(2,1)S(1)}, bf16[768,192]{0,1:T(8,128)(2,1)}, u32[]{:S(2)}) copy-start(bf16[768,192]{0,1:T(8,128)(2,1)} %param.20) | copy-start | bytes 884740
  168.8 7.6 %copy-start.72 = (f32[192]{0:T(256)S(1)}, f32[192]{0:T(256)}, u32[]{:S(2)}) copy-start(f32[192]{0:T(256)} %param.22) | copy-start | bytes 2308
  194.5 6.4 %copy-start.2 = (bf16[192,38,134]{2,1,0:T(8,128)(2,1)S(1)}, bf16[192,38,134]{2,1,0:T(8,128)(2,1)}, u32[]{:S(2)}) copy-start(bf16[192,38,134]{2,1,0:T(8,128)(2,1)} %select_maximum_fusion.2) | copy-start | bytes 5865988
  257.0 35.3 %copy-start.91 = (f32[192]{0:T(256)S(1)}, f32[192]{0:T(256)}, u32[]{:S(2)}) copy-start(f32[192]{0:T(256)} %get-tuple-element.46) | copy-start | bytes 2308
  257.0 37.5 %copy-start.90 = (f32[192]{0:T(256)S(1)}, f32[192]{0:T(256)}, u32[]{:S(2)}) copy-start(f32[192]{0:T(256)} %get-tuple-element.45) | copy-start | bytes 2308
  257.0 38.2 %copy-start.89 = (f32[192]{0:T(256)S(1)}, f32[192]{0:T(256)}, u32[]{:S(2)}) copy-start(f32[192]{0:T(256)} %get-tuple-element.44) | copy-start | bytes 2308
  257.0 39.0 %copy-start.88 = (f32[192]{0:T(256)S(1)}, f32[192]{0:T(256)}, u32[]{:S(2)}) copy-start(f32[192]{0:T(256)} %get-tuple-element.43) | copy-start | bytes 2308
  257.1 39.7 %copy-start.87 = (f32[192]{0:T(256)S(1)}, f32[192]{0:T(256)}, u32[]{:S(2)}) copy-start(f32[192]{0:T(256)} %get-tuple-element.42) | copy-start | bytes 2308
  257.1 40.5 %copy-start.86 = (f32[192]{0:T(256)S(1)}, f32[192]{0:T(256)}, u32[]{:S(2)}) copy-start(f32[192]{0:T(256)} %get-tuple-element.41) | copy-start | bytes 2308
  257.1 41.3 %copy-start.85 = (f32[192]{0:T(256)S(1)}, f32[192]{0:T(256)}, u32[]{:S(2)}) copy-start(f32[192]{0:T(256)} %get-tuple-element.40) | copy-start | bytes 2308
  257.1 43.5 %copy-start.84 = (f32[192]{0:T(256)S(1)}, f32[192]{0:T(256)}, u32[]{:S(2)}) copy-start(f32[192]{0:T(256)} %get-tuple-element.39) | copy-start | bytes 2308
  257.1 44.2 %copy-start.83 = (f32[192]{0:T(256)S(1)}, f32[192]{0:T(256)}, u32[]{:S(2)}) copy-start(f32[192]{0:T(256)} %get-tuple-element.38) | copy-start | bytes 2308
  257.1 45.0 %copy-start.82 = (f32[192]{0:T(256)S(1)}, f32[192]{0:T(256)}, u32[]{:S(2)}) copy-start(f32[192]{0:T(256)} %get-tuple-element.37) | copy-start | bytes 2308
  257.1 45.7 %copy-start.81 = (f32[192]{0:T(256)S(1)}, f32[192]{0:T(256)}, u32[]{:S(2)}) copy-start(f32[192]{0:T(256)} %get-tuple-element.36) | copy-start | bytes 2308
  257.1 46.5 %copy-start.80 = (f32[192]{0:T(256)S(1)}, f32[192]{0:T(256)}, u32[]{:S(2)}) copy-start(f32[192]{0:T(256)} %get-tuple-element.35) | copy-start | bytes 2308
  257.1 47.2 %copy-start.79 = (f32[192]{0:T(256)S(1)}, f32[192]{0:T(256)}, u32[]{:S(2)}) copy-start(f32[192]{0:T(256)} %get-tuple-element.34) | copy-start | bytes 2308
  257.1 49.4 %copy-start.78 = (f32[192]{0:T(256)S(1)}, f32[192]{0:T(256)}, u32[]{:S(2)}) copy-start(f32[192]{0:T(256)} %get-tuple-element.33) | copy-start | bytes 2308
  268.6 38.7 %copy-start.77 = (f32[192]{0:T(256)S(1)}, f32[192]{0:T(256)}, u32[]{:S(2)}) copy-start(f32[192]{0:T(256)} %get-tuple-element.32) | copy-start | bytes 2308
  268.6 39.5 %copy-start.76 = (f32[192]{0:T(256)S(1)}, f32[192]{0:T(256)}, u32[]{:S(2)}) copy-start(f32[192]{0:T(256)} %get-tuple-element.31) | copy-start | bytes 2308
  268.6 40.3 %copy-start.75 = (f32[192]{0:T(256)S(1)}, f32[192]{0:T(256)}, u32[]{:S(2)}) copy-start(f32[192]{0:T(256)} %get-tuple-element.30) | copy-start | bytes 2308
  268.6 41.0 %copy-start.74 = (f32[192]{0:T(256)S(1)}, f32[192]{0:T(256)}, u32[]{:S(2)}) copy-start(f32[192]{0:T(256)} %get-tuple-element.29) | copy-start | bytes 2308
  268.6 46.9 %copy-start.11 = (f32[1,192,768]{2,1,0:T(8,128)S(1)}, f32[1,192,768]{2,1,0:T(8,128)}, u32[]{:S(2)}) copy-start(f32[1,192,768]{2,1,0:T(8,128)} %convolution_bitcast_fusion.1) | copy-start | bytes 1769476
  343.5 7.6 %collective-permute-start.3 = (bf16[192,3,128]{2,1,0:T(4,128)(2,1)S(1)}, bf16[192,3,128]{2,1,0:T(4,128)(2,1)S(1)}, u32[]{:S(2)}, u32[]{:S(2)}) collective-permute-start(bf16[192,3,128]{2,1,0:T(4,128)(2,1)S(1)} %get-tuple-element.80), channel_id=1, source_target_pairs={{1,0},{2,1},{3,2},{4,3},{5,4},{6,5},{7,6},{9,8},{10,9},{11,10},{12... | collective-permute-start | bytes 442376 | tf_op jit(solution)/shard_map/ppermute | solution.py:20
  344.8 8.3 %collective-permute-start.2 = (bf16[192,3,128]{2,1,0:T(4,128)(2,1)S(1)}, bf16[192,3,128]{2,1,0:T(4,128)(2,1)S(1)}, u32[]{:S(2)}, u32[]{:S(2)}) collective-permute-start(bf16[192,3,128]{2,1,0:T(4,128)(2,1)S(1)} %get-tuple-element.79), channel_id=1, source_target_pairs={{0,1},{1,2},{2,3},{3,4},{4,5},{5,6},{6,7},{8,9},{9,10},{10,11},{11... | collective-permute-start | bytes 442376 | tf_op jit(solution)/shard_map/ppermute | solution.py:18
  350.2 6.2 %copy-start.15 = (f32[192,1]{0,1:T(1,128)S(1)}, f32[192,1]{0,1:T(1,128)}, u32[]{:S(2)}) copy-start(f32[192,1]{0,1:T(1,128)} %copy-done.14) | copy-start | bytes 2308
  350.2 6.2 %copy-start.17 = (f32[192,1]{0,1:T(1,128)S(1)}, f32[192,1]{0,1:T(1,128)}, u32[]{:S(2)}) copy-start(f32[192,1]{0,1:T(1,128)} %copy-done.16) | copy-start | bytes 2308
  350.3 6.2 %copy-start.19 = (f32[192,1]{0,1:T(1,128)S(1)}, f32[192,1]{0,1:T(1,128)}, u32[]{:S(2)}) copy-start(f32[192,1]{0,1:T(1,128)} %copy-done.18) | copy-start | bytes 2308
  350.3 6.2 %copy-start.21 = (f32[192,1]{0,1:T(1,128)S(1)}, f32[192,1]{0,1:T(1,128)}, u32[]{:S(2)}) copy-start(f32[192,1]{0,1:T(1,128)} %copy-done.20) | copy-start | bytes 2308
  350.3 6.2 %copy-start.23 = (f32[192,1]{0,1:T(1,128)S(1)}, f32[192,1]{0,1:T(1,128)}, u32[]{:S(2)}) copy-start(f32[192,1]{0,1:T(1,128)} %copy-done.22) | copy-start | bytes 2308
  350.3 6.2 %copy-start.25 = (f32[192,1]{0,1:T(1,128)S(1)}, f32[192,1]{0,1:T(1,128)}, u32[]{:S(2)}) copy-start(f32[192,1]{0,1:T(1,128)} %copy-done.24) | copy-start | bytes 2308
  350.3 6.2 %copy-start.27 = (f32[192,1]{0,1:T(1,128)S(1)}, f32[192,1]{0,1:T(1,128)}, u32[]{:S(2)}) copy-start(f32[192,1]{0,1:T(1,128)} %copy-done.26) | copy-start | bytes 2308
  350.3 6.2 %copy-start.29 = (f32[192,1]{0,1:T(1,128)S(1)}, f32[192,1]{0,1:T(1,128)}, u32[]{:S(2)}) copy-start(f32[192,1]{0,1:T(1,128)} %copy-done.28) | copy-start | bytes 2308
  350.3 6.2 %copy-start.31 = (f32[192,1]{0,1:T(1,128)S(1)}, f32[192,1]{0,1:T(1,128)}, u32[]{:S(2)}) copy-start(f32[192,1]{0,1:T(1,128)} %copy-done.30) | copy-start | bytes 2308
  350.3 6.2 %copy-start.33 = (f32[192,1]{0,1:T(1,128)S(1)}, f32[192,1]{0,1:T(1,128)}, u32[]{:S(2)}) copy-start(f32[192,1]{0,1:T(1,128)} %copy-done.32) | copy-start | bytes 2308
  350.3 6.2 %copy-start.35 = (f32[192,1]{0,1:T(1,128)S(1)}, f32[192,1]{0,1:T(1,128)}, u32[]{:S(2)}) copy-start(f32[192,1]{0,1:T(1,128)} %copy-done.34) | copy-start | bytes 2308
  350.3 6.2 %copy-start.37 = (f32[192,1]{0,1:T(1,128)S(1)}, f32[192,1]{0,1:T(1,128)}, u32[]{:S(2)}) copy-start(f32[192,1]{0,1:T(1,128)} %copy-done.36) | copy-start | bytes 2308
  350.4 6.2 %copy-start.39 = (f32[192,1]{0,1:T(1,128)S(1)}, f32[192,1]{0,1:T(1,128)}, u32[]{:S(2)}) copy-start(f32[192,1]{0,1:T(1,128)} %copy-done.38) | copy-start | bytes 2308
  350.4 6.2 %copy-start.41 = (f32[192,1]{0,1:T(1,128)S(1)}, f32[192,1]{0,1:T(1,128)}, u32[]{:S(2)}) copy-start(f32[192,1]{0,1:T(1,128)} %copy-done.40) | copy-start | bytes 2308
  555.7 16.7 %copy-start.1 = (bf16[192,768]{1,0:T(8,128)(2,1)S(1)}, bf16[192,768]{1,0:T(8,128)(2,1)}, u32[]{:S(2)}) copy-start(bf16[192,768]{1,0:T(8,128)(2,1)} %param.18) | copy-start | bytes 884740
  (37 other events, 197.4 us)
Sparse Core Ops, SparseCore 0:
  323.0 232.5 all-gather.1
